TPU v7x, 128 devices: a whole 4x4x4 slice. The times are simulated.
128 devices in a mesh: grp: 8 (over z_hi, x), ep: 8 (over y, core), tp: 2 (over z_lo).
Axes of the slice: x: 4, y: 4, z: 4 (z_hi: 2, z_lo: 2; z = z_hi * 2 + z_lo), core: 2. Of those that a mesh axis runs over, the one named last changes fastest.
Arguments:
- residual: bfloat16 [2048, 4096], P(('grp', 'ep'), 'tp'), may hold values from -400 to 400
- queries: bfloat16 [2048, 4096], P(('grp', 'ep'), 'tp'), may hold values from -8 to 8
- token_key_value: bfloat16 [2048, 2, 1024], P(('grp', 'ep'), None, 'tp'), may hold values from -4 to 4
- cache: bfloat16 [2048, 2, 192, 1024], P(('grp', 'ep'), None, None, 'tp'), may hold values from -8 to 8
- cache_length: int32 [2048], P(('grp', 'ep')), may hold values from 2 to 192, as said below
- active: int32 [2048], P(('grp', 'ep')), may hold values from 0 to 1, as said below
- routes: int32 [2048, 2], P(('grp', 'ep')), may hold values from 0 to 7, as said below
- norm_gain: bfloat16 [4096], P('tp'), may hold values from 0.099609375 to 1.8984375
- router: bfloat16 [4096, 8], P('tp'), may hold values from -0.09375 to 0.09375
- w_gate: bfloat16 [8, 4096, 8192], P('ep', ('grp', 'tp')), may hold values from -0.09375 to 0.09375
- w_up: bfloat16 [8, 4096, 8192], P('ep', ('grp', 'tp')), may hold values from -0.09375 to 0.09375
- w_down: bfloat16 [8, 4096, 8192], P('ep', ('grp', 'tp')), may hold values from -0.0625 to 0.0625
Outputs:
- delta: bfloat16 [2048, 4096], P(('grp', 'ep'), 'tp')
Inputs may be any that keep to these rules, and one draw needn't show every extreme that they name: `cache_length`: every device's 32 sequences include one with 192 cached positions. The sequences that name their group's common expert first (see routes) all have active = 1. `routes`: each sequence names two different experts; among the sequences of one device no expert is named more than 16 times, and one expert, the same for every device of a grp index, is named first by exactly 16 of each such device's sequences.
All inputs are finite; a program needn't handle non-finite values.
Results may differ from a plain program's by a relative error of at most 0.012.
Values may be sent and summed in bfloat16 or wider, within the bound.
A program may use at most 192 MiB of HBM per device.

v0:
```python
import jax
import jax.numpy as jnp
from jax import lax
from jax.sharding import PartitionSpec as P

MODEL_WIDTH = 4096
QUERY_HEADS = 32
KEY_VALUE_HEADS = 8
HEAD_SIZE = 128
EPSILON = 1e-05


def attend_local(queries, token_key_value, cache, cache_length):
    seq_count = queries.shape[0]
    positions = cache.shape[2]
    heads_kv = cache.shape[3] // HEAD_SIZE
    group_share = QUERY_HEADS // KEY_VALUE_HEADS
    score_scale = HEAD_SIZE ** (-0.5)
    query_head_rows = queries.reshape(seq_count, heads_kv, group_share, HEAD_SIZE)
    stored_keys = cache[:, 0].reshape(seq_count, positions, heads_kv, HEAD_SIZE)
    stored_values = cache[:, 1].reshape(seq_count, positions, heads_kv, HEAD_SIZE)
    incoming_key = token_key_value[:, 0].reshape(seq_count, heads_kv, HEAD_SIZE)
    incoming_value = token_key_value[:, 1].reshape(seq_count, heads_kv, HEAD_SIZE)
    scores = (
        jnp.einsum(
            "skgd,slkd->skgl", query_head_rows, stored_keys, preferred_element_type=jnp.float32
        )
        * score_scale
    )
    in_cache = (
        jnp.arange(positions, dtype=jnp.int32)[None, None, None, :]
        < cache_length[:, None, None, None]
    )
    scores = jnp.where(in_cache, scores, -jnp.inf)
    self_score = (
        jnp.einsum(
            "skgd,skd->skg", query_head_rows, incoming_key, preferred_element_type=jnp.float32
        )
        * score_scale
    )
    highest = jnp.maximum(jnp.max(scores, axis=-1), self_score)
    exponent = jnp.exp(scores - highest[..., None])
    own_exp = jnp.exp(self_score - highest)
    totals = jnp.sum(exponent, axis=-1) + own_exp
    normalized = (exponent / totals[..., None]).astype(jnp.bfloat16)
    own_weight = (own_exp / totals).astype(jnp.bfloat16)
    mixture = jnp.einsum(
        "skgl,slkd->skgd", normalized, stored_values, preferred_element_type=jnp.float32
    )
    mixture = (
        mixture
        + own_weight.astype(jnp.float32)[..., None]
        * incoming_value.astype(jnp.float32)[:, :, None, :]
    )
    return mixture.reshape(seq_count, heads_kv * group_share * HEAD_SIZE).astype(jnp.bfloat16)


def per_device(
    residual,
    queries,
    token_key_value,
    cache,
    cache_length,
    active,
    routes,
    norm_gain,
    router,
    w_gate,
    w_up,
    w_down,
):
    tp_count = lax.axis_size("tp")
    tp_rank = lax.axis_index("tp")
    gate_serve, up_serve = (
        lax.all_to_all(w_gate, ("grp", "tp"), split_axis=2, concat_axis=1, tiled=True),
        lax.all_to_all(w_up, ("grp", "tp"), split_axis=2, concat_axis=1, tiled=True),
    )
    attention_output = attend_local(queries, token_key_value, cache, cache_length)
    state = residual.astype(jnp.float32) + attention_output.astype(jnp.float32)
    scaled = state * norm_gain.astype(jnp.float32)[None, :]
    squares, raw_logits = lax.psum(
        (
            jnp.sum(state * state, axis=1),
            jnp.dot(scaled, router.astype(jnp.float32), precision=lax.Precision.HIGHEST),
        ),
        "tp",
    )
    row_scale = jnp.sqrt(squares / MODEL_WIDTH + EPSILON)[:, None]
    logits = raw_logits / row_scale
    normed = lax.all_gather((scaled / row_scale).astype(jnp.bfloat16), "tp", axis=1, tiled=True)
    chosen = jnp.take_along_axis(logits, routes, axis=1)
    weight_first = jax.nn.sigmoid(chosen[:, 0] - chosen[:, 1])
    weight_second = 1.0 - weight_first
    seq_count = residual.shape[0]
    expert_count = router.shape[1]
    half_cap = seq_count // 2 // tp_count
    slot_total = half_cap * expert_count
    still_live = active == 1
    flat_expert = routes.reshape(-1)
    flat_live = jnp.repeat(still_live, 2)
    onehot = (
        (flat_expert[:, None] == jnp.arange(expert_count, dtype=jnp.int32)[None, :])
        & flat_live[:, None]
    ).astype(jnp.int32)
    before = jnp.cumsum(onehot, axis=0) - onehot
    rank_order = jnp.sum(before * onehot, axis=1)
    owner_half = rank_order // half_cap
    slot_index = rank_order % half_cap * expert_count + flat_expert
    on_this_half = flat_live & (owner_half == tp_rank)
    selector = (
        (
            (slot_index[:, None] == jnp.arange(slot_total, dtype=jnp.int32)[None, :])
            & on_this_half[:, None]
        )
        .astype(jnp.bfloat16)
        .reshape(seq_count, 2, slot_total)
    )
    senders = selector[:, 0] + selector[:, 1]
    outgoing = lax.dot_general(
        senders, normed, (((0,), (0,)), ((), ())), preferred_element_type=jnp.float32
    )
    outgoing = outgoing.astype(jnp.bfloat16).reshape(half_cap, expert_count, normed.shape[1])
    arrived = lax.all_to_all(outgoing, "ep", split_axis=1, concat_axis=0, tiled=True)
    portion = lax.all_gather(arrived, ("grp", "tp"), axis=0, tiled=True)
    gate_part = jnp.einsum("red,edf->ref", portion, gate_serve, preferred_element_type=jnp.float32)
    up_part = jnp.einsum("red,edf->ref", portion, up_serve, preferred_element_type=jnp.float32)
    hidden = (jax.nn.silu(gate_part) * up_part).astype(jnp.bfloat16)
    partial_sums = jnp.einsum(
        "ref,edf->red",
        lax.all_gather(hidden, ("grp", "tp"), axis=2, tiled=True),
        w_down,
        preferred_element_type=jnp.float32,
    )
    results = lax.all_to_all(
        partial_sums.astype(jnp.bfloat16), ("grp", "tp"), split_axis=0, concat_axis=2, tiled=True
    )
    returned = lax.all_to_all(results, "ep", split_axis=0, concat_axis=1, tiled=True).reshape(
        slot_total, normed.shape[1]
    )
    pick_first = jnp.dot(selector[:, 0], returned, preferred_element_type=jnp.float32)
    pick_second = jnp.dot(selector[:, 1], returned, preferred_element_type=jnp.float32)
    combined = weight_first[:, None] * pick_first + weight_second[:, None] * pick_second
    moe_sum = lax.psum_scatter(
        combined.astype(jnp.bfloat16), "tp", scatter_dimension=1, tiled=True
    ).astype(jnp.float32)
    delta = jnp.where(still_live[:, None], attention_output.astype(jnp.float32) + moe_sum, 0.0)
    return delta.astype(jnp.bfloat16)


def solution(mesh):
    in_specs = (
        P(("grp", "ep"), "tp"),
        P(("grp", "ep"), "tp"),
        P(("grp", "ep"), None, "tp"),
        P(("grp", "ep"), None, None, "tp"),
        P(("grp", "ep")),
        P(("grp", "ep")),
        P(("grp", "ep"), None),
        P("tp"),
        P("tp", None),
        P("ep", ("grp", "tp"), None),
        P("ep", ("grp", "tp"), None),
        P("ep", ("grp", "tp"), None),
    )
    out_specs = P(("grp", "ep"), "tp")
    return jax.shard_map(
        per_device, mesh=mesh, in_specs=in_specs, out_specs=out_specs, check_vma=False
    )
```

profile of v0, /device:TPU:1, one launch (start us, length us, event | category | flops | bytes accessed | tf_op | source)
XLA Modules:
  0.0 794.2 jit_solution(5515043613989613150)
XLA Ops:
  6.5 10.5 %fusion.74 = (bf16[32,1,192,512]{3,2,1,0:T(8,128)(2,1)}, bf16[32,1,192,512]{3,2,1,0:T(8,128)(2,1)}) fusion(bf16[32,2,192,512]{3,2,1,0:T(8,128)(2,1)} %param.15), kind=kLoop, calls=%fused_computation.95 | loop fusion | bytes 25165824 | tf_op jit(solution)/shard_map/slice | solution.py:20
  17.1 9.8 %reshape_squeeze.10 = bf16[32,192,4,128]{3,2,1,0:T(4,128)(2,1)} reshape(bf16[32,1,192,512]{3,2,1,0:T(8,128)(2,1)} %get-tuple-element.9) | data formatting | bytes 12582912 | tf_op jit(solution)/shard_map/reshape;squeeze | solution.py:20
  27.4 6.2 fusion.75
  34.2 9.8 %reshape_squeeze.12 = bf16[32,192,4,128]{3,2,1,0:T(4,128)(2,1)} reshape(bf16[32,1,192,512]{3,2,1,0:T(8,128)(2,1)} %get-tuple-element.10) | data formatting | bytes 12582912 | tf_op jit(solution)/shard_map/reshape;squeeze | solution.py:21
  49.1 4.9 all-reduce
  60.5 16.5 %all_to_all.82 = bf16[8,8,4096]{2,0,1:T(8,128)(2,1)} all-to-all(bf16[8,8,4096]{2,0,1:T(8,128)(2,1)S(1)} %copy.90), channel_id=1, replica_groups=mesh['grp'=8,'ep'=8,'tp'=2] {'ep'}, dimensions={1} | all-to-all | bytes 1048576 | tf_op jit(solution)/shard_map/all_to_all | solution.py:123
  77.0 18.0 %copy.91 = bf16[1,256,8192]{1,0,2:T(2,128)(2,1)} copy(bf16[1,256,8192]{2,1,0:T(8,128)(2,1)} %param.21) | data formatting | bytes 8388608 | tf_op args[9]
  95.5 43.5 %reduce.4 = bf16[8192,256]{1,0:T(8,128)(2,1)} reduce(bf16[8192,1,256]{2,1,0:T(2,128)(2,1)} %bitcast.117, bf16[]{:T(256)} %broadcast.143), dimensions={1}, to_apply=%bitcast.106.reduce_sub_computation | reduce | bytes 8388610
  138.9 10.5 %reshape.180 = bf16[16,2,65536]{2,1,0:T(2,128)(2,1)} reshape(bf16[8192,256]{1,0:T(8,128)(2,1)} %reduce.4) | data formatting | bytes 8388608
  149.4 7.7 all-to-all-start.1
  157.1 17.9 %copy.93 = bf16[1,256,8192]{1,0,2:T(2,128)(2,1)} copy(bf16[1,256,8192]{2,1,0:T(8,128)(2,1)} %param.22) | data formatting | bytes 8388608 | tf_op args[10]
  175.0 43.5 %reduce.5 = bf16[8192,256]{1,0:T(8,128)(2,1)} reduce(bf16[8192,1,256]{2,1,0:T(2,128)(2,1)} %bitcast.120, bf16[]{:T(256)} %broadcast.143), dimensions={1}, to_apply=%bitcast.108.reduce_sub_computation | reduce | bytes 8388610
  218.5 10.5 %reshape.182 = bf16[16,2,65536]{2,1,0:T(2,128)(2,1)} reshape(bf16[8192,256]{1,0:T(8,128)(2,1)} %reduce.5) | data formatting | bytes 8388608
  229.0 8.5 %all-to-all-done.1 = bf16[16,2,65536]{2,1,0:T(2,128)(2,1)} async-done(((bf16[16,2,65536]{2,1,0:T(2,128)(2,1)}), bf16[16,2,65536]{2,1,0:T(2,128)(2,1)}, u32[]{:S(2)}, u32[]{:S(2)}) %all-to-all-start.1) | async-done | bytes 4194336 | tf_op jit(solution)/shard_map/all_to_all | solution.py:75
  237.5 10.9 %all-to-all-start.2 = ((bf16[16,2,65536]{2,1,0:T(2,128)(2,1)}), bf16[16,2,65536]{2,1,0:T(2,128)(2,1)}, u32[]{:S(2)}, u32[]{:S(2)}) async-start(bf16[16,2,65536]{2,1,0:T(2,128)(2,1)} %reshape.182), calls=%async_computation.2 | async-start | bytes 8388608 | tf_op jit(solution)/shard_map/all_to_all | solution.py:76
  248.5 12.4 %reshape.181 = bf16[8192,1,256]{2,1,0:T(2,128)(2,1)} reshape(bf16[16,2,65536]{2,1,0:T(2,128)(2,1)} %all-to-all-done.1) | data formatting | bytes 8388608
  260.9 6.1 copy.101
  266.9 6.4 copy.92
  273.3 50.0 %all-to-all-done.2 = bf16[16,2,65536]{2,1,0:T(2,128)(2,1)} async-done(((bf16[16,2,65536]{2,1,0:T(2,128)(2,1)}), bf16[16,2,65536]{2,1,0:T(2,128)(2,1)}, u32[]{:S(2)}, u32[]{:S(2)}) %all-to-all-start.2) | async-done | bytes 4194336 | tf_op jit(solution)/shard_map/all_to_all | solution.py:76
  323.3 12.4 %reshape.183 = bf16[8192,1,256]{2,1,0:T(2,128)(2,1)} reshape(bf16[16,2,65536]{2,1,0:T(2,128)(2,1)} %all-to-all-done.2) | data formatting | bytes 8388608
  335.7 6.1 copy.102
  341.8 6.4 copy.94
  348.2 5.4 all-gather.3.cloned.1.call-done
  353.7 8.5 %fusion.4 = f32[1024,512]{1,0:T(8,128)S(1)} fusion(bf16[4096,512]{1,0:T(8,128)(2,1)} %bitcast.125, bf16[1024,1,4096]{2,0,1:T(8,128)(2,1)} %all-gather.3.cloned.1.call-done), kind=kOutput, calls=%fused_computation.5 | convolution fusion | flops 4294967296 | bytes 14680064 | tf_op jit(solution)/shard_map/red,edf->ref/dot_general | solution.py:125
  362.2 5.7 fusion.14
  367.9 347.5 %all-gather.5.cloned.1.call-done = bf16[1024,1,8192]{2,0,1:T(8,128)(2,1)} async-done(((bf16[1024,1,512]{2,0,1:T(8,128)(2,1)}), bf16[1024,1,8192]{2,0,1:T(8,128)(2,1)}) %all-gather.5.cloned.1.call-update) | async-done | bytes 16777232 | tf_op jit(solution)/shard_map/all_gather | solution.py:130
  715.5 11.5 %fusion.25 = bf16[1024,1,256]{2,0,1:T(8,128)(2,1)S(1)} fusion(bf16[1,256,8192]{2,1,0:T(8,128)(2,1)} %param.23, bf16[1024,1,8192]{2,0,1:T(8,128)(2,1)} %all-gather.5.cloned.1.call-done), kind=kOutput, calls=%fused_computation.26 | convolution fusion | flops 4295229440 | bytes 21495808 | tf_op jit(solution)/shard_map/ref,edf->red/dot_general | solution.py:128
  728.9 11.3 %all-to-all-start.3 = ((bf16[16,2,8192]{2,1,0:T(2,128)(2,1)}), bf16[16,2,8192]{2,1,0:T(2,128)(2,1)S(1)}, u32[]{:S(2)}, u32[]{:S(2)}) async-start(bf16[16,2,8192]{2,1,0:T(2,128)(2,1)} %reshape.184), calls=%async_computation.3 | async-start | bytes 1048576 | tf_op jit(solution)/shard_map/all_to_all | solution.py:134
  740.8 10.2 %all-to-all-done.3 = bf16[16,2,8192]{2,1,0:T(2,128)(2,1)S(1)} async-done(((bf16[16,2,8192]{2,1,0:T(2,128)(2,1)}), bf16[16,2,8192]{2,1,0:T(2,128)(2,1)S(1)}, u32[]{:S(2)}, u32[]{:S(2)}) %all-to-all-start.3) | async-done | bytes 524320 | tf_op jit(solution)/shard_map/all_to_all | solution.py:134
  757.4 6.0 all-to-all-start.4
  764.5 8.3 %all-to-all-done.4 = bf16[8,2,16384]{2,1,0:T(2,128)(2,1)S(1)} async-done(((bf16[8,2,16384]{2,1,0:T(2,128)(2,1)}), bf16[8,2,16384]{2,1,0:T(2,128)(2,1)S(1)}, u32[]{:S(2)}, u32[]{:S(2)}) %all-to-all-start.4) | async-done | bytes 524320 | tf_op jit(solution)/shard_map/all_to_all | solution.py:137
  775.5 10.6 %reduce-scatter.2.cloned.1.call-done = bf16[32,2048]{1,0:T(8,128)(2,1)} async-done(((bf16[32,4096]{1,0:T(8,128)(2,1)}), bf16[32,2048]{1,0:T(8,128)(2,1)}) %reduce-scatter.2.cloned.1.call-update) | async-done | bytes 131088 | tf_op jit(solution)/shard_map/reduce_scatter | solution.py:143
  (87 shorter events, 27.4 us)
Async XLA Ops:
  6.5 42.4 %copy-start = (bf16[2048,8]{0,1:T(8,128)(2,1)S(1)}, bf16[2048,8]{0,1:T(8,128)(2,1)}, u32[]{:S(2)}) copy-start(bf16[2048,8]{0,1:T(8,128)(2,1)} %param.20) | copy-start | bytes 98308
  6.5 347.1 %all-gather.3.cloned.1.call-start = ((), (), s32[]{:S(2)}) async-start(), calls=%async_computation.6 | async-start | bytes 8912896 | tf_op jit(solution)/shard_map/all_gather | solution.py:124
  17.1 9.8 %copy-start.4 = (bf16[32,2048]{1,0:T(8,128)(2,1)S(1)}, bf16[32,2048]{1,0:T(8,128)(2,1)}, u32[]{:S(2)}) copy-start(bf16[32,2048]{1,0:T(8,128)(2,1)} %param.13) | copy-start | bytes 393220
  17.1 9.9 %copy-start.8 = (s32[32]{0:T(128)S(1)}, s32[32]{0:T(128)}, u32[]{:S(2)}) copy-start(s32[32]{0:T(128)} %param.16) | copy-start | bytes 388
  17.1 10.0 %copy-start.5 = (bf16[32,2,512]{2,1,0:T(2,128)(2,1)S(1)}, bf16[32,2,512]{2,1,0:T(2,128)(2,1)}, u32[]{:S(2)}) copy-start(bf16[32,2,512]{2,1,0:T(2,128)(2,1)} %param.14) | copy-start | bytes 196612
  44.0 4.8 copy-start.6
  44.0 4.8 copy-start.3
  44.0 10.0 %copy-start.7 = (s32[32,2]{0,1:T(2,128)S(1)}, s32[32,2]{0,1:T(2,128)}, u32[]{:S(2)}) copy-start(s32[32,2]{0,1:T(2,128)} %param.18) | copy-start | bytes 772
  44.0 10.2 %copy-start.10 = (s32[32]{0:T(128)S(1)}, s32[32]{0:T(128)}, u32[]{:S(2)}) copy-start(s32[32]{0:T(128)} %param.17) | copy-start | bytes 388
  149.4 88.1 %all-to-all-start.1 = ((bf16[16,2,65536]{2,1,0:T(2,128)(2,1)}), bf16[16,2,65536]{2,1,0:T(2,128)(2,1)}, u32[]{:S(2)}, u32[]{:S(2)}) async-start(bf16[16,2,65536]{2,1,0:T(2,128)(2,1)} %reshape.180), calls=%async_computation.1 | async-start | bytes 8388608 | tf_op jit(solution)/shard_map/all_to_all | solution.py:75
  237.5 85.8 %all-to-all-start.2 = ((bf16[16,2,65536]{2,1,0:T(2,128)(2,1)}), bf16[16,2,65536]{2,1,0:T(2,128)(2,1)}, u32[]{:S(2)}, u32[]{:S(2)}) async-start(bf16[16,2,65536]{2,1,0:T(2,128)(2,1)} %reshape.182), calls=%async_computation.2 | async-start | bytes 8388608 | tf_op jit(solution)/shard_map/all_to_all | solution.py:76
  248.4 467.1 %all-gather.5.cloned.1.call-start = ((), (), s32[]{:S(2)}) async-start(), calls=%async_computation.7 | async-start | bytes 17825792 | tf_op jit(solution)/shard_map/all_gather | solution.py:130
  353.7 8.5 %copy-start.2 = (bf16[1,16,256,512]{3,2,1,0:T(8,128)(2,1)S(1)}, bf16[1,16,256,512]{3,2,1,0:T(8,128)(2,1)}, u32[]{:S(2)}) copy-start(bf16[1,16,256,512]{3,2,1,0:T(8,128)(2,1)} %copy.94) | copy-start | bytes 12582916
  353.7 8.5 %copy-start.9 = (bf16[1024,1,4096]{2,0,1:T(8,128)(2,1)S(1)}, bf16[1024,1,4096]{2,0,1:T(8,128)(2,1)}, u32[]{:S(2)}) copy-start(bf16[1024,1,4096]{2,0,1:T(8,128)(2,1)} %all-gather.3.cloned.1.call-done) | copy-start | bytes 25165828
  728.9 22.0 %all-to-all-start.3 = ((bf16[16,2,8192]{2,1,0:T(2,128)(2,1)}), bf16[16,2,8192]{2,1,0:T(2,128)(2,1)S(1)}, u32[]{:S(2)}, u32[]{:S(2)}) async-start(bf16[16,2,8192]{2,1,0:T(2,128)(2,1)} %reshape.184), calls=%async_computation.3 | async-start | bytes 1048576 | tf_op jit(solution)/shard_map/all_to_all | solution.py:134
  757.4 15.4 %all-to-all-start.4 = ((bf16[8,2,16384]{2,1,0:T(2,128)(2,1)}), bf16[8,2,16384]{2,1,0:T(2,128)(2,1)S(1)}, u32[]{:S(2)}, u32[]{:S(2)}) async-start(bf16[8,2,16384]{2,1,0:T(2,128)(2,1)} %reshape.186), calls=%async_computation.4 | async-start | bytes 1048576 | tf_op jit(solution)/shard_map/all_to_all | solution.py:137
  763.4 22.6 %reduce-scatter.2.cloned.1.call-start = ((), (), s32[]{:S(2)}) async-start(), calls=%async_computation.8 | async-start | bytes 393216 | tf_op jit(solution)/shard_map/reduce_scatter | solution.py:143
  763.4 24.3 %copy-start.1 = (bf16[2048,8]{0,1:T(8,128)(2,1)S(1)}, bf16[2048,8]{0,1:T(8,128)(2,1)}, u32[]{:S(2)}) copy-start(bf16[2048,8]{0,1:T(8,128)(2,1)} %param.20) | copy-start | bytes 98308
Sparse Core Ops, SparseCore 0:
  77.1 276.5 all-gather.2
  368.1 347.3 all-gather.4
  775.6 10.3 reduce-scatter.1
where the time goes:
time: 797 us; the launch traced here: 794 us
  waiting for transfers between devices  441 us (55%)
  local copies, waits for them, and re-layouts  144 us (18%)
  other arithmetic  95.3 us (12%)
  matrix products  39 us (5%)
  starting transfers between devices  36 us (5%)
  blocking collectives  25.8 us (3%)
  between operations  13.4 us (2%)
    all_gather x1, waiting for transfers between devices, per_device(): lax.all_gather(hidden, ('grp', 'tp'), axis=2, tiled=True)  348 us
    unnamed x38, local copies, waits for them, and re-layouts  98.4 us
    unnamed x2, other arithmetic  86.9 us
    all_to_all x1, waiting for transfers between devices, per_device(): lax.all_to_all(w_up, ('grp', 'tp'), split_axis=2, concat_axis=1, tiled=True)  50 us
    all_to_all x1, blocking collectives, per_device(): lax.all_to_all(outgoing, 'ep', split_axis=1, concat_axis=0, tiled=True)  16.5 us
  transfers between devices with their start and end apart: 7, of which 7 were waited for; matrix products, arithmetic and copies ran while one was open for 25% of the time, Pallas kernels for 0%

commit v1 on v0

--- a/solution.py
+++ b/solution.py
@@ -8,6 +8,11 @@
 KEY_VALUE_HEADS = 8
 HEAD_SIZE = 128
 EPSILON = 1e-05
+
+
+def swapped_in(x, mesh_axis, dim):
+    outgoing = jnp.stack([x] * lax.axis_size(mesh_axis))
+    return jnp.concatenate(lax.all_to_all(outgoing, mesh_axis, 0, 0), axis=dim)
 
 
 def attend_local(queries, token_key_value, cache, cache_length):
@@ -127,7 +132,7 @@
     hidden = (jax.nn.silu(gate_part) * up_part).astype(jnp.bfloat16)
     partial_sums = jnp.einsum(
         "ref,edf->red",
-        lax.all_gather(hidden, ("grp", "tp"), axis=2, tiled=True),
+        swapped_in(hidden, ("grp", "tp"), 2),
         w_down,
         preferred_element_type=jnp.float32,
     )

time: 797 us -> 638 us (0.80)
  waiting for transfers between devices: 441 us -> 92.8 us
  blocking collectives: 25.8 us -> 217 us
    all_gather x1 -> x0, waiting for transfers between devices: 348 us -> none  [per_device(): lax.all_gather(hidden, ('grp', 'tp'), axis=2, tiled=True)]
    all_to_all x0 -> x1, blocking collectives: none -> 191 us  [swapped_in(): return jnp.concatenate(lax.all_to_all(outgoing, mesh_axis, 0, 0), axis=dim)]
    unnamed x38 -> x28, local copies, waits for them, and re-layouts: 98.4 us -> 99 us
  transfers between devices with their start and end apart: 7 -> 6, of which waited for: 7 -> 6; matrix products, arithmetic and copies ran while one was open for 25% -> 31% of each run, Pallas kernels for 0% -> 0%
where the time goes in v1:
time: 638 us; the launch traced here: 635 us
  blocking collectives  217 us (34%)
  local copies, waits for them, and re-layouts  148 us (23%)
  other arithmetic  98.8 us (15%)
  waiting for transfers between devices  92.8 us (15%)
  matrix products  33.9 us (5%)
  starting transfers between devices  30.1 us (5%)
  between operations  13.7 us (2%)
    all_to_all x1, blocking collectives, swapped_in(): return jnp.concatenate(lax.all_to_all(outgoing, mesh_axis, 0, 0), axis=dim)  191 us
    unnamed x28, local copies, waits for them, and re-layouts  99 us
    unnamed x2, other arithmetic  86.9 us
    all_to_all x1, waiting for transfers between devices, per_device(): lax.all_to_all(w_up, ('grp', 'tp'), split_axis=2, concat_axis=1, tiled=True)  49.6 us
    all_to_all x1, blocking collectives, per_device(): lax.all_to_all(outgoing, 'ep', split_axis=1, concat_axis=0, tiled=True)  16.5 us
  transfers between devices with their start and end apart: 6, of which 6 were waited for; matrix products, arithmetic and copies ran while one was open for 31% of the time, Pallas kernels for 0%

profile of v1, /device:TPU:1, one launch (start us, length us, event | category | flops | bytes accessed | tf_op | source)
XLA Modules:
  0.0 634.9 jit_solution(2411806057443314665)
XLA Ops:
  14.2 10.5 %fusion.72 = (bf16[32,1,192,512]{3,2,1,0:T(8,128)(2,1)}, bf16[32,1,192,512]{3,2,1,0:T(8,128)(2,1)}) fusion(bf16[32,2,192,512]{3,2,1,0:T(8,128)(2,1)} %param.15), kind=kLoop, calls=%fused_computation.95 | loop fusion | bytes 25165824 | tf_op jit(solution)/shard_map/slice | solution.py:25
  24.7 9.7 %reshape_squeeze.10 = bf16[32,192,4,128]{3,2,1,0:T(4,128)(2,1)} reshape(bf16[32,1,192,512]{3,2,1,0:T(8,128)(2,1)} %get-tuple-element.9) | data formatting | bytes 12582912 | tf_op jit(solution)/shard_map/reshape;squeeze | solution.py:25
  34.4 6.2 fusion.73
  41.2 9.8 %reshape_squeeze.12 = bf16[32,192,4,128]{3,2,1,0:T(4,128)(2,1)} reshape(bf16[32,1,192,512]{3,2,1,0:T(8,128)(2,1)} %get-tuple-element.10) | data formatting | bytes 12582912 | tf_op jit(solution)/shard_map/reshape;squeeze | solution.py:26
  56.1 4.9 all-reduce
  66.3 16.5 %all_to_all.87 = bf16[8,8,4096]{2,0,1:T(8,128)(2,1)} all-to-all(bf16[8,8,4096]{2,0,1:T(8,128)(2,1)S(1)} %copy.94), channel_id=1, replica_groups=mesh['grp'=8,'ep'=8,'tp'=2] {'ep'}, dimensions={1} | all-to-all | bytes 1048576 | tf_op jit(solution)/shard_map/all_to_all | solution.py:128
  82.8 18.0 %copy.95 = bf16[1,256,8192]{1,0,2:T(2,128)(2,1)} copy(bf16[1,256,8192]{2,1,0:T(8,128)(2,1)} %param.21) | data formatting | bytes 8388608 | tf_op args[9]
  101.3 43.5 %reduce.5 = bf16[8192,256]{1,0:T(8,128)(2,1)} reduce(bf16[8192,1,256]{2,1,0:T(2,128)(2,1)} %bitcast.124, bf16[]{:T(256)} %broadcast.146), dimensions={1}, to_apply=%bitcast.114.reduce_sub_computation | reduce | bytes 8388610
  144.7 10.5 %reshape.191 = bf16[16,2,65536]{2,1,0:T(2,128)(2,1)} reshape(bf16[8192,256]{1,0:T(8,128)(2,1)} %reduce.5) | data formatting | bytes 8388608
  155.2 7.7 %all-to-all-start.1 = ((bf16[16,2,65536]{2,1,0:T(2,128)(2,1)}), bf16[16,2,65536]{2,1,0:T(2,128)(2,1)}, u32[]{:S(2)}, u32[]{:S(2)}) async-start(bf16[16,2,65536]{2,1,0:T(2,128)(2,1)} %reshape.191), calls=%async_computation.1 | async-start | bytes 8388608 | tf_op jit(solution)/shard_map/all_to_all | solution.py:80
  162.9 17.9 %copy.97 = bf16[1,256,8192]{1,0,2:T(2,128)(2,1)} copy(bf16[1,256,8192]{2,1,0:T(8,128)(2,1)} %param.22) | data formatting | bytes 8388608 | tf_op args[10]
  180.9 43.5 %reduce.4 = bf16[8192,256]{1,0:T(8,128)(2,1)} reduce(bf16[8192,1,256]{2,1,0:T(2,128)(2,1)} %bitcast.127, bf16[]{:T(256)} %broadcast.146), dimensions={1}, to_apply=%bitcast.112.reduce_sub_computation | reduce | bytes 8388610
  224.3 10.5 %reshape.189 = bf16[16,2,65536]{2,1,0:T(2,128)(2,1)} reshape(bf16[8192,256]{1,0:T(8,128)(2,1)} %reduce.4) | data formatting | bytes 8388608
  234.8 8.6 %all-to-all-done.1 = bf16[16,2,65536]{2,1,0:T(2,128)(2,1)} async-done(((bf16[16,2,65536]{2,1,0:T(2,128)(2,1)}), bf16[16,2,65536]{2,1,0:T(2,128)(2,1)}, u32[]{:S(2)}, u32[]{:S(2)}) %all-to-all-start.1) | async-done | bytes 4194336 | tf_op jit(solution)/shard_map/all_to_all | solution.py:80
  243.4 10.9 %all-to-all-start.2 = ((bf16[16,2,65536]{2,1,0:T(2,128)(2,1)}), bf16[16,2,65536]{2,1,0:T(2,128)(2,1)}, u32[]{:S(2)}, u32[]{:S(2)}) async-start(bf16[16,2,65536]{2,1,0:T(2,128)(2,1)} %reshape.189), calls=%async_computation.2 | async-start | bytes 8388608 | tf_op jit(solution)/shard_map/all_to_all | solution.py:81
  254.2 12.4 %reshape.192 = bf16[8192,1,256]{2,1,0:T(2,128)(2,1)} reshape(bf16[16,2,65536]{2,1,0:T(2,128)(2,1)} %all-to-all-done.1) | data formatting | bytes 8388608
  266.6 6.1 copy.107
  272.7 6.4 %copy.96 = bf16[1,16,256,512]{3,2,1,0:T(8,128)(2,1)} copy(bf16[1,16,256,512]{2,3,1,0:T(8,128)(2,1)} %bitcast.128) | data formatting | bytes 8388608 | tf_op jit(solution)/shard_map/all_to_all | solution.py:80
  279.1 49.6 %all-to-all-done.2 = bf16[16,2,65536]{2,1,0:T(2,128)(2,1)} async-done(((bf16[16,2,65536]{2,1,0:T(2,128)(2,1)}), bf16[16,2,65536]{2,1,0:T(2,128)(2,1)}, u32[]{:S(2)}, u32[]{:S(2)}) %all-to-all-start.2) | async-done | bytes 4194336 | tf_op jit(solution)/shard_map/all_to_all | solution.py:81
  328.7 12.4 %reshape.190 = bf16[8192,1,256]{2,1,0:T(2,128)(2,1)} reshape(bf16[16,2,65536]{2,1,0:T(2,128)(2,1)} %all-to-all-done.2) | data formatting | bytes 8388608
  341.1 6.1 copy.108
  347.2 6.4 %copy.98 = bf16[1,16,256,512]{3,2,1,0:T(8,128)(2,1)} copy(bf16[1,16,256,512]{2,3,1,0:T(8,128)(2,1)} %bitcast.129) | data formatting | bytes 8388608 | tf_op jit(solution)/shard_map/all_to_all | solution.py:81
  353.6 6.1 all-gather.2.cloned.1.call-done
  359.7 8.3 %fusion.2 = f32[1024,512]{1,0:T(8,128)S(1)} fusion(bf16[4096,512]{1,0:T(8,128)(2,1)} %bitcast.133, bf16[1024,1,4096]{2,0,1:T(8,128)(2,1)} %all-gather.2.cloned.1.call-done), kind=kOutput, calls=%fused_computation.3 | convolution fusion | flops 4294967296 | bytes 14680064 | tf_op jit(solution)/shard_map/red,edf->ref/dot_general | solution.py:130
  368.0 4.7 fusion.19
  375.4 191.4 %all_to_all.88 = bf16[16,1024,1,512]{1,3,2,0:T(8,128)(2,1)S(1)} all-to-all(bf16[16,1024,1,512]{1,3,2,0:T(8,128)(2,1)S(1)} %stack.2), channel_id=1, replica_groups=mesh['grp'=8,'ep'=8,'tp'=2] {'grp','tp'}, dimensions={0} | all-to-all | bytes 33554432 | tf_op jit(solution)/shard_map/all_to_all | solution.py:15
  566.8 6.9 %fusion.25 = bf16[1024,1,256]{2,0,1:T(8,128)(2,1)S(1)} fusion(bf16[1024,8192]{0,1:T(8,128)(2,1)S(1)} %bitcast.130, bf16[1,256,8192]{2,1,0:T(8,128)(2,1)} %param.23), kind=kOutput, calls=%fused_computation.26 | convolution fusion | flops 4295229440 | bytes 21495808 | tf_op jit(solution)/shard_map/ref,edf->red/dot_general | solution.py:133
  575.6 5.1 all-to-all-start.4
  581.2 9.6 %all-to-all-done.4 = bf16[16,2,8192]{2,1,0:T(2,128)(2,1)S(1)} async-done(((bf16[16,2,8192]{2,1,0:T(2,128)(2,1)}), bf16[16,2,8192]{2,1,0:T(2,128)(2,1)S(1)}, u32[]{:S(2)}, u32[]{:S(2)}) %all-to-all-start.4) | async-done | bytes 524320 | tf_op jit(solution)/shard_map/all_to_all | solution.py:139
  597.3 6.5 %all-to-all-start.5 = ((bf16[8,2,16384]{2,1,0:T(2,128)(2,1)}), bf16[8,2,16384]{2,1,0:T(2,128)(2,1)S(1)}, u32[]{:S(2)}, u32[]{:S(2)}) async-start(bf16[8,2,16384]{2,1,0:T(2,128)(2,1)} %reshape.195), calls=%async_computation.5 | async-start | bytes 1048576 | tf_op jit(solution)/shard_map/all_to_all | solution.py:142
  604.9 8.3 %all-to-all-done.5 = bf16[8,2,16384]{2,1,0:T(2,128)(2,1)S(1)} async-done(((bf16[8,2,16384]{2,1,0:T(2,128)(2,1)}), bf16[8,2,16384]{2,1,0:T(2,128)(2,1)S(1)}, u32[]{:S(2)}, u32[]{:S(2)}) %all-to-all-start.5) | async-done | bytes 524320 | tf_op jit(solution)/shard_map/all_to_all | solution.py:142
  615.9 10.6 %reduce-scatter.2.cloned.1.call-done = bf16[32,2048]{1,0:T(8,128)(2,1)} async-done(((bf16[32,4096]{1,0:T(8,128)(2,1)}), bf16[32,2048]{1,0:T(8,128)(2,1)}) %reduce-scatter.2.cloned.1.call-update) | async-done | bytes 131088 | tf_op jit(solution)/shard_map/reduce_scatter | solution.py:148
  (77 shorter events, 36.0 us)
Async XLA Ops:
  6.5 49.4 %copy-start = (bf16[2048,8]{0,1:T(8,128)(2,1)S(1)}, bf16[2048,8]{0,1:T(8,128)(2,1)}, u32[]{:S(2)}) copy-start(bf16[2048,8]{0,1:T(8,128)(2,1)} %param.20) | copy-start | bytes 98308
  6.5 353.1 %all-gather.2.cloned.1.call-start = ((), (), s32[]{:S(2)}) async-start(), calls=%async_computation.7 | async-start | bytes 8912896 | tf_op jit(solution)/shard_map/all_gather | solution.py:129
  51.0 4.8 copy-start.3
  155.2 88.1 %all-to-all-start.1 = ((bf16[16,2,65536]{2,1,0:T(2,128)(2,1)}), bf16[16,2,65536]{2,1,0:T(2,128)(2,1)}, u32[]{:S(2)}, u32[]{:S(2)}) async-start(bf16[16,2,65536]{2,1,0:T(2,128)(2,1)} %reshape.191), calls=%async_computation.1 | async-start | bytes 8388608 | tf_op jit(solution)/shard_map/all_to_all | solution.py:80
  243.4 85.3 %all-to-all-start.2 = ((bf16[16,2,65536]{2,1,0:T(2,128)(2,1)}), bf16[16,2,65536]{2,1,0:T(2,128)(2,1)}, u32[]{:S(2)}, u32[]{:S(2)}) async-start(bf16[16,2,65536]{2,1,0:T(2,128)(2,1)} %reshape.189), calls=%async_computation.2 | async-start | bytes 8388608 | tf_op jit(solution)/shard_map/all_to_all | solution.py:81
  359.7 8.3 %copy-start.2 = (bf16[1,16,256,512]{3,2,1,0:T(8,128)(2,1)S(1)}, bf16[1,16,256,512]{3,2,1,0:T(8,128)(2,1)}, u32[]{:S(2)}) copy-start(bf16[1,16,256,512]{3,2,1,0:T(8,128)(2,1)} %copy.98) | copy-start | bytes 12582916
  359.7 8.3 %copy-start.5 = (bf16[1024,1,4096]{2,0,1:T(8,128)(2,1)S(1)}, bf16[1024,1,4096]{2,0,1:T(8,128)(2,1)}, u32[]{:S(2)}) copy-start(bf16[1024,1,4096]{2,0,1:T(8,128)(2,1)} %all-gather.2.cloned.1.call-done) | copy-start | bytes 25165828
  566.8 13.9 %copy-start.4 = (s32[32,2]{0,1:T(2,128)S(1)}, s32[32,2]{0,1:T(2,128)}, u32[]{:S(2)}) copy-start(s32[32,2]{0,1:T(2,128)} %param.18) | copy-start | bytes 772
  575.6 15.2 %all-to-all-start.4 = ((bf16[16,2,8192]{2,1,0:T(2,128)(2,1)}), bf16[16,2,8192]{2,1,0:T(2,128)(2,1)S(1)}, u32[]{:S(2)}, u32[]{:S(2)}) async-start(bf16[16,2,8192]{2,1,0:T(2,128)(2,1)} %reshape.193), calls=%async_computation.4 | async-start | bytes 1048576 | tf_op jit(solution)/shard_map/all_to_all | solution.py:139
  597.3 15.9 %all-to-all-start.5 = ((bf16[8,2,16384]{2,1,0:T(2,128)(2,1)}), bf16[8,2,16384]{2,1,0:T(2,128)(2,1)S(1)}, u32[]{:S(2)}, u32[]{:S(2)}) async-start(bf16[8,2,16384]{2,1,0:T(2,128)(2,1)} %reshape.195), calls=%async_computation.5 | async-start | bytes 1048576 | tf_op jit(solution)/shard_map/all_to_all | solution.py:142
  603.8 22.6 %reduce-scatter.2.cloned.1.call-start = ((), (), s32[]{:S(2)}) async-start(), calls=%async_computation.8 | async-start | bytes 393216 | tf_op jit(solution)/shard_map/reduce_scatter | solution.py:148
  603.8 24.3 %copy-start.1 = (bf16[2048,8]{0,1:T(8,128)(2,1)S(1)}, bf16[2048,8]{0,1:T(8,128)(2,1)}, u32[]{:S(2)}) copy-start(bf16[2048,8]{0,1:T(8,128)(2,1)} %param.20) | copy-start | bytes 98308
Sparse Core Ops, SparseCore 0:
  82.9 276.7 all-gather.1
  616.0 10.3 reduce-scatter.1
